TPU v7x, 32 devices: a whole 2x2x4 slice. The times are simulated.
32 devices in a mesh: seq: 8 (over y, x, core), head: 4 (over z).
Axes of the slice: x: 2, y: 2, z: 4, core: 2. Of those that a mesh axis runs over, the one named last changes fastest.
Arguments:
- inputs: bfloat16 [2048, 4096], P('seq'), may hold values from -6 to 6
- x_weight: bfloat16 [4096, 8192], P('seq', 'head'), may hold values from -0.125 to 0.125
- b_values: bfloat16 [2048, 8, 128], P('seq'), may hold values from -0.5 to 0.5
- c_values: bfloat16 [2048, 8, 128], P('seq'), may hold values from -0.375 to 0.375
- gate_z: bfloat16 [2048, 8192], P('seq', 'head'), may hold values from -6 to 6
- log_decay: float32 [2048, 128], P('seq', 'head'), may hold values from -2 to 0
- skip_gain: float32 [128], P('head'), may hold values from 0.5 to 1.5
- grad_out: bfloat16 [2048, 8192], P('seq', 'head'), may hold values from -6 to 6
Outputs:
- input_grad: bfloat16 [2048, 4096], P('seq', 'head')
- z_grad: bfloat16 [2048, 8192], P('seq', 'head')
All inputs are finite; a program needn't handle non-finite values.
Results may differ from a plain program's by a relative error of at most 0.0095.
Values may be sent and summed in bfloat16 or wider, within the bound.
A program may use at most 128 MiB of HBM per device.

v0:
```python
import jax
import jax.numpy as jnp
from jax import lax
from jax.sharding import PartitionSpec as P

HEADS = 128
HEAD_DIM = 64
STATE = 128
GROUPS = 8
SPAN = 256
EXACT_MODE = lax.Precision.HIGHEST


def prefix_2(array, axis, combine, identity):
    size, place = (lax.axis_size(axis), lax.axis_index(axis))
    everything = jax.tree.map(
        lambda part, kind: lax.all_gather(part.astype(kind), axis),
        array,
        (jnp.bfloat16, jnp.bfloat16),
    )
    start = jax.tree.map(
        lambda part, zero: jnp.broadcast_to(jnp.asarray(zero, part.dtype), part.shape),
        array,
        identity,
    )

    def prefix_hop(k, before):
        reached = k < place
        new = combine(
            before, jax.tree.map(lambda part, own: part[k].astype(own.dtype), everything, array)
        )
        return jax.tree.map(lambda a, b: jnp.where(reached, a, b), new, before)

    return lax.fori_loop(0, size, prefix_hop, start)


def entering(value, axis, join, neutral):
    count, mine = (lax.axis_size(axis), lax.axis_index(axis))
    pieces = jax.tree.map(lambda part: lax.all_gather(part, axis), value)
    pieces = jax.tree.map(lambda part: part[::-1], pieces)
    mine = count - 1 - mine
    so_far = jax.tree.map(
        lambda part, zero: jnp.full_like(part, 0) + jnp.asarray(zero, part.dtype), value, neutral
    )

    def entering_hop(position, so_far):
        longer = join(so_far, jax.tree.map(lambda part: part[position], pieces))
        return jax.tree.map(lambda new, old: jnp.where(position < mine, new, old), longer, so_far)

    return lax.fori_loop(0, count - 1, entering_hop, so_far)


def decayed_scores(c_block, b_block, prefix):
    scores = jnp.einsum("thn,shn->hts", c_block, b_block, preferred_element_type=jnp.float32)
    later = prefix.T[:, :, None]
    earlier = prefix.T[:, None, :]
    positions = jnp.arange(prefix.shape[0])
    causal = (positions[:, None] >= positions[None, :])[None, :, :]
    spacing = jnp.where(causal, later - earlier, 0.0)
    factors = jnp.where(causal, jnp.exp(spacing), 0.0)
    return (scores * factors).astype(jnp.bfloat16)


def compose(earlier, later):
    return (earlier[0] * later[0], later[0][:, None, None] * earlier[1] + later[1])


def body(inputs, x_weight, b_values, c_values, gate_z, log_decay, skip_gain, grad_out):
    token_count = inputs.shape[0]
    head_count = log_decay.shape[1]
    width_here = x_weight.shape[1]
    block_count = token_count // SPAN
    full_weight = lax.all_gather(x_weight, "seq", axis=0, tiled=True)
    x_sums = jnp.dot(inputs, full_weight, preferred_element_type=jnp.float32)
    x_values = x_sums.astype(jnp.bfloat16)
    first_head = lax.axis_index("head") * head_count
    owners = (first_head + jnp.arange(head_count)) // (HEADS // GROUPS)
    picker = (owners[:, None] == jnp.arange(GROUPS)[None, :]).astype(jnp.bfloat16)
    b_heads = jnp.einsum(
        "tgn,hg->thn", b_values, picker, preferred_element_type=jnp.float32
    ).astype(jnp.bfloat16)
    c_heads = jnp.einsum(
        "tgn,hg->thn", c_values, picker, preferred_element_type=jnp.float32
    ).astype(jnp.bfloat16)
    x_blocks = x_values.reshape(block_count, SPAN, head_count, HEAD_DIM)
    b_blocks = b_heads.reshape(block_count, SPAN, head_count, STATE)
    c_blocks = c_heads.reshape(block_count, SPAN, head_count, STATE)
    prefix = jnp.cumsum(log_decay.reshape(block_count, SPAN, head_count), axis=1)
    totals = prefix[:, -1, :]
    gate = gate_z.astype(jnp.float32).reshape(token_count, head_count, HEAD_DIM)
    upstream = grad_out.astype(jnp.float32).reshape(token_count, head_count, HEAD_DIM)
    sigma = jax.nn.sigmoid(gate)
    y_grad = upstream * gate * sigma
    grad_blocks = y_grad.reshape(block_count, SPAN, head_count, HEAD_DIM)
    low_blocks = grad_blocks.astype(jnp.bfloat16)
    tails = jnp.exp(totals[:, None, :] - prefix)
    fresh_states = jnp.einsum(
        "kshp,kshn->khpn",
        x_blocks.astype(jnp.float32) * tails[..., None],
        b_blocks.astype(jnp.float32),
        precision=EXACT_MODE,
    )
    fresh_grads = jnp.einsum(
        "kthp,kthn->khpn",
        grad_blocks * jnp.exp(prefix)[..., None],
        c_blocks.astype(jnp.float32),
        precision=EXACT_MODE,
    )
    running = jnp.cumsum(totals, axis=0)
    after = running[-1][None, :] - running
    before = running - totals
    device_decay = jnp.exp(running[-1])
    device_state = jnp.einsum("kh,khpn->hpn", jnp.exp(after), fresh_states, precision=EXACT_MODE)
    device_grad = jnp.einsum("kh,khpn->hpn", jnp.exp(before), fresh_grads, precision=EXACT_MODE)
    unit_decay = jnp.ones((head_count,), jnp.float32)
    start_state = prefix_2(
        (device_decay, device_state), "seq", compose, (unit_decay, jnp.zeros_like(device_state))
    )[1]
    end_grad = entering(
        (device_decay, device_grad), "seq", compose, (unit_decay, jnp.zeros_like(device_grad))
    )[1]
    gain = skip_gain[None, :, None]

    def forward(state, items):
        x_block, b_block, c_block, prefix_block, fresh = items
        weights = decayed_scores(c_block, b_block, prefix_block)
        local = jnp.einsum("hts,shp->thp", weights, x_block, preferred_element_type=jnp.float32)
        carried = jnp.exp(prefix_block)[:, :, None] * jnp.einsum(
            "thn,hpn->thp", c_block.astype(jnp.float32), state, precision=EXACT_MODE
        )
        state = jnp.exp(prefix_block[-1])[:, None, None] * state + fresh
        return (state, (local + carried + gain * x_block.astype(jnp.float32), weights))

    final_state, (outputs, weight_blocks) = lax.scan(
        forward, start_state, (x_blocks, b_blocks, c_blocks, prefix, fresh_states)
    )
    outputs = outputs.reshape(token_count, head_count, HEAD_DIM)
    z_grad = (upstream * outputs * sigma * (1.0 + gate * (1.0 - sigma))).astype(jnp.bfloat16)
    z_grad = z_grad.reshape(token_count, width_here)

    def backward(carry, items):
        weights, b_block, tail_block, total_block, grad_block, low_block, fresh = items
        local = jnp.einsum("hts,thp->shp", weights, low_block, preferred_element_type=jnp.float32)
        carried = tail_block[:, :, None] * jnp.einsum(
            "shn,hpn->shp", b_block.astype(jnp.float32), carry, precision=EXACT_MODE
        )
        carry = jnp.exp(total_block)[:, None, None] * carry + fresh
        return (carry, local + carried + gain * grad_block)

    final_grad, x_grads = lax.scan(
        backward,
        end_grad,
        (weight_blocks, b_blocks, tails, totals, grad_blocks, low_blocks, fresh_grads),
        reverse=True,
    )
    x_grad = x_grads.reshape(token_count, width_here).astype(jnp.bfloat16)
    partial_sums = jnp.einsum("tk,dk->td", x_grad, full_weight, preferred_element_type=jnp.float32)
    input_grad = lax.psum_scatter(
        partial_sums.astype(jnp.bfloat16), "head", scatter_dimension=1, tiled=True
    )
    return (input_grad, z_grad)


def solution(mesh):
    in_specs = (
        P("seq", None),
        P("seq", "head"),
        P("seq", None, None),
        P("seq", None, None),
        P("seq", "head"),
        P("seq", "head"),
        P("head"),
        P("seq", "head"),
    )
    out_specs = (P("seq", "head"), P("seq", "head"))
    return jax.shard_map(body, mesh=mesh, in_specs=in_specs, out_specs=out_specs, check_vma=False)
```

profile of v0, /device:TPU:0, one launch (start us, length us, event | category | flops | bytes accessed | tf_op | source)
XLA Modules:
  0.0 324.2 jit_solution(4623977196892682287)
XLA Ops:
  9.8 2.0 convert_bitcast_fusion
  11.9 90.6 %all-gather.8.cloned.1.call-done = bf16[4096,2048]{1,0:T(8,128)(2,1)} async-done(((bf16[512,2048]{1,0:T(8,128)(2,1)}), bf16[4096,2048]{1,0:T(8,128)(2,1)}) %all-gather.8.cloned.1.call-update) | async-done | bytes 16777232 | tf_op jit(solution)/shard_map/all_gather | solution.py:73
  102.5 8.3 %convolution_convert_fusion.1 = bf16[256,2048]{1,0:T(8,128)(2,1)S(1)} fusion(bf16[256,4096]{1,0:T(8,128)(2,1)S(1)} %copy-done, bf16[4096,2048]{1,0:T(8,128)(2,1)} %all-gather.8.cloned.1.call-done), kind=kOutput, calls=%fused_computation.14 | convolution fusion | flops 4295491584 | bytes 19922944 | tf_op jit(solution)/shard_map/dot_general | solution.py:74
  111.5 4.3 %fusion.32 = bf16[32,64,128]{2,1,0:T(8,128)(2,1)} fusion(bf16[256,32,128]{2,1,0:T(8,128)(2,1)} %convert_bitcast_fusion, bf16[256,32,64]{0,2,1:T(8,128)(2,1)S(1)} %bitcast.101, f32[256,32]{0,1:T(8,128)S(1)} %copy-done.8, f32[32]{0:T(128)S(1)} %subtract_exponential_fusion), kind=kOutput, calls=%fused_computation.43 | convolution fusion | flops 806879232 | bytes 3702912 | tf_op jit(solution)/shard_map/kshp,kshn->khpn/dot_general | solution.py:97
  116.0 8.9 %all-gather.3 = bf16[8,1,32]{2,1,0:T(2,128)(2,1)S(1)} all-gather(bf16[1,1,32]{2,1,0:T(2,128)(2,1)S(1)} %get-tuple-element.325), channel_id=5, replica_groups=mesh['seq'=8,'head'=4] {'seq'}, dimensions={0}, use_global_device_ids=true | all-gather | bytes 576 | tf_op jit(solution)/shard_map/all_gather | solution.py:17
  126.6 6.0 %multiply_convert_fusion = bf16[32,256,256]{2,1,0:T(8,128)(2,1)S(1)} fusion(f32[32,256]{1,0:T(8,128)S(1)} %copy.73, pred[256,256]{1,0:T(8,128)(4,1)S(1)} %iota_compare_fusion, bf16[256,32,128]{2,1,0:T(8,128)(2,1)S(1)} %copy-done.4, bf16[256,32,128]{2,1,0:T(8,128)(2,1)S(1)} %convert_bitcast_fusion.1), kind=kOutput, calls=%fused_computation.6 | convolution fusion | flops 547356672 | bytes 8486912 | tf_op jit(solution)/shard_map/while/body/eval_jaxpr/thn,shn->hts/dot_general | solution.py:54
  132.7 2.0 copy-done.3
  134.6 2.7 fusion.45
  137.4 15.4 %all-gather.12.cloned.1.call-done = bf16[256,64,128]{2,1,0:T(8,128)(2,1)} async-done(((bf16[32,64,128]{2,1,0:T(8,128)(2,1)}), bf16[256,64,128]{2,1,0:T(8,128)(2,1)}) %all-gather.12.cloned.1.call-update) | async-done | bytes 4194320 | tf_op jit(solution)/shard_map/all_gather | solution.py:17
  152.8 10.7 %while.19 = (s32[]{:T(128)}, f32[32,64,128]{2,1,0:T(8,128)S(1)}, s32[]{:T(128)}, bf16[8,32]{1,0:T(8,128)(2,1)S(1)}, bf16[8,32,64,128]{3,2,1,0:T(8,128)(2,1)}, /*index=5*/s32[]{:T(128)}, s32[]{:T(128)}) while((s32[]{:T(128)}, f32[32,64,128]{2,1,0:T(8,128)S(1)}, s32[]{:T(128)}, bf16[8,32]{1,0:T(8,128)(2,1)S(1)}, ...), condition=%wide.region_6.7_spmd.clone, body=%wide.region_5.6_spmd.clone.sunk | while | flops 1310756 | bytes 2621873 | solution.py:34
  158.1 1.3 fusion.61
  162.1 1.3 fusion.61
  163.5 6.3 %fusion.6 = f32[256,32,64]{0,2,1:T(8,128)} fusion(bf16[256,32,64]{0,2,1:T(8,128)(2,1)S(1)} %bitcast.103, f32[32,64,256]{2,1,0:T(8,128)} %fusion.45, f32[32,64,128]{2,1,0:T(8,128)S(1)} %get-tuple-element.254, bf16[256,32,128]{2,1,0:T(8,128)(2,1)} %copy-done.2, f32[256,32]{0,1:T(8,128)S(1)} %copy.80, f32[32]{0:T(128)S(1)} %copy-done.11), kind=kOutput, calls=%fused_computation.19 | convolution fusion | flops 807927808 | bytes 8421504 | tf_op jit(solution)/shard_map/while/body/eval_jaxpr/thn,hpn->thp/dot_general | solution.py:128
  169.8 2.0 copy.83
  171.8 3.9 %fusion.4 = (bf16[256,2048]{1,0:T(8,128)(2,1)}, f32[256,2048]{1,0:T(8,128)}) fusion(f32[256,2048]{1,0:T(8,128)S(1)} %copy.83, bf16[256,2048]{1,0:T(8,128)(2,1)S(1)} %copy-done.5, bf16[256,2048]{1,0:T(8,128)(2,1)} %param.16), kind=kLoop, calls=%fused_computation.17 | loop fusion | flops 7340032 | bytes 7340032 | tf_op jit(solution)/shard_map/convert_element_type | solution.py:138
  175.7 1.9 copy.67
  177.6 4.5 %fusion.24 = f32[32,64,128]{2,1,0:T(8,128)} fusion(bf16[256,32,128]{2,1,0:T(8,128)(2,1)} %copy-done.2, f32[256,32,64]{0,2,1:T(8,128)S(1)} %bitcast.98, f32[256,32]{0,1:T(8,128)S(1)} %copy.76, f32[32]{0:T(128)S(1)} %subtract_exponential_fusion), kind=kOutput, calls=%fused_computation.41 | convolution fusion | flops 806092800 | bytes 5275776 | tf_op jit(solution)/shard_map/kthp,kthn->khpn/dot_general | solution.py:103
  182.3 8.9 %all-gather = f32[8,1,32]{2,1,0:T(1,128)S(1)} all-gather(f32[1,1,32]{2,1,0:T(1,128)S(1)} %get-tuple-element.327), channel_id=2, replica_groups=mesh['seq'=8,'head'=4] {'seq'}, dimensions={0}, use_global_device_ids=true | all-gather | bytes 1152 | tf_op jit(solution)/shard_map/all_gather | solution.py:39
  191.2 4.5 %fusion.37 = f32[32,64,256]{2,1,0:T(8,128)} fusion(bf16[32,256,256]{2,1,0:T(8,128)(2,1)} %copy-done.3, f32[256,32,64]{0,2,1:T(8,128)S(1)} %bitcast.99), kind=kOutput, calls=%fused_computation.46 | convolution fusion | flops 268959744 | bytes 8388608 | tf_op jit(solution)/shard_map/while/body/eval_jaxpr/hts,thp->shp/dot_general | solution.py:143
  195.7 41.1 %all-gather.10.cloned.1.call-done = f32[256,64,128]{2,1,0:T(8,128)} async-done(((f32[32,64,128]{2,1,0:T(8,128)}), f32[256,64,128]{2,1,0:T(8,128)}) %all-gather.10.cloned.1.call-update) | async-done | bytes 8388624 | tf_op jit(solution)/shard_map/all_gather | solution.py:39
  236.7 8.3 %rev.7 = f32[8,32,64,128]{3,2,1,0:T(8,128)} reverse(f32[8,32,64,128]{3,2,1,0:T(8,128)} %bitcast.104), dimensions={0} | reverse | bytes 16777216 | tf_op jit(solution)/shard_map/rev | solution.py:40
  245.0 10.5 %while.18 = (s32[]{:T(128)}, f32[32,64,128]{2,1,0:T(8,128)S(1)}, s32[]{:T(128)}, f32[8,32]{1,0:T(8,128)S(1)}, f32[8,32,64,128]{3,2,1,0:T(8,128)}, /*index=5*/s32[]{:T(128)}, s32[]{:T(128)}) while((s32[]{:T(128)}, f32[32,64,128]{2,1,0:T(8,128)S(1)}, s32[]{:T(128)}, f32[8,32]{1,0:T(8,128)S(1)}, f32[8,32,64,128]{3,2,1,0:T(8,128)}, ...), condition=%wide.region_3.4_spmd.clone, body=%wide.region_2.3_spmd.clone.sunk | while | flops 1048580 | bytes 3146225 | solution.py:50
  245.0 1.5 fusion.60
  246.5 1.5 fusion.60
  248.0 1.5 fusion.60
  249.6 1.5 fusion.60
  251.1 1.5 fusion.60
  252.6 1.5 fusion.60
  254.1 1.5 fusion.60
  255.6 5.9 %fusion.15 = bf16[256,32,64]{0,2,1:T(8,128)(2,1)} fusion(f32[32,64,256]{2,1,0:T(8,128)} %fusion.37, f32[256,32,64]{0,2,1:T(8,128)S(1)} %bitcast.100, f32[32,64,128]{2,1,0:T(8,128)S(1)} %get-tuple-element.253, bf16[256,32,128]{2,1,0:T(8,128)(2,1)} %convert_bitcast_fusion, f32[32]{0:T(128)S(1)} %copy-done.11, f32[256,32]{0,1:T(8,128)S(1)} %copy-done.9), kind=kOutput, calls=%fused_computation.30 | convolution fusion | flops 807927808 | bytes 8421504 | tf_op jit(solution)/shard_map/while/body/eval_jaxpr/shn,hpn->shp/dot_general | solution.py:144
  261.5 12.1 %convolution_convert_fusion = bf16[256,4096]{1,0:T(8,128)(2,1)} fusion(bf16[256,2048]{0,1:T(8,128)(2,1)} %bitcast.110, bf16[4096,2048]{1,0:T(8,128)(2,1)} %all-gather.8.cloned.1.call-done), kind=kOutput, calls=%fused_computation.7 | convolution fusion | flops 4296015872 | bytes 19922944 | tf_op jit(solution)/shard_map/tk,dk->td/dot_general | solution.py:157
  273.6 44.0 %reduce-scatter.2.cloned.1.call-done = bf16[256,1024]{1,0:T(8,128)(2,1)} async-done(((bf16[256,4096]{1,0:T(8,128)(2,1)}), bf16[256,1024]{1,0:T(8,128)(2,1)}) %reduce-scatter.2.cloned.1.call-update) | async-done | bytes 524304 | tf_op jit(solution)/shard_map/reduce_scatter | solution.py:158
  (75 shorter events, 13.2 us)
Async XLA Ops:
  7.2 95.4 %copy-start = (bf16[256,4096]{1,0:T(8,128)(2,1)S(1)}, bf16[256,4096]{1,0:T(8,128)(2,1)}, u32[]{:S(2)}) copy-start(bf16[256,4096]{1,0:T(8,128)(2,1)} %param.12) | copy-start | bytes 6291460
  7.2 0.9 copy-start.10
  7.2 2.6 copy-start.6
  7.2 95.3 %all-gather.8.cloned.1.call-start = ((), (), s32[]{:S(2)}) async-start(), calls=%async_computation.1 | async-start | bytes 18874368 | tf_op jit(solution)/shard_map/all_gather | solution.py:73
  7.9 144.8 %all-gather.12.cloned.1.call-start = ((), (), s32[]{:S(2)}) async-start(), calls=%async_computation.4 | async-start | bytes 4718592 | tf_op jit(solution)/shard_map/all_gather | solution.py:17
  110.8 0.8 copy-start.8
  111.5 13.5 %copy-start.7 = (bf16[256,8,128]{2,1,0:T(8,128)(2,1)S(1)}, bf16[256,8,128]{2,1,0:T(8,128)(2,1)}, u32[]{:S(2)}) copy-start(bf16[256,8,128]{2,1,0:T(8,128)(2,1)} %param.15) | copy-start | bytes 1572868
  115.9 120.9 %all-gather.10.cloned.1.call-start = ((), (), s32[]{:S(2)}) async-start(), calls=%async_computation.3 | async-start | bytes 9437184 | tf_op jit(solution)/shard_map/all_gather | solution.py:39
  125.0 1.6 copy-start.4
  126.6 6.0 %copy-start.2 = (bf16[256,32,128]{2,1,0:T(8,128)(2,1)}, bf16[256,32,128]{2,1,0:T(8,128)(2,1)S(1)}, u32[]{:S(2)}) copy-start(bf16[256,32,128]{2,1,0:T(8,128)(2,1)S(1)} %convert_bitcast_fusion.1) | copy-start | bytes 6291460
  132.6 2.0 copy-start.3
  152.8 10.7 %copy-start.11 = (f32[32]{0:T(128)S(1)}, f32[32]{0:T(128)}, u32[]{:S(2)}) copy-start(f32[32]{0:T(128)} %param.18) | copy-start | bytes 388
  169.8 2.0 copy-start.5
  182.2 135.5 %reduce-scatter.2.cloned.1.call-start = ((), (), s32[]{:S(2)}) async-start(), calls=%async_computation.2 | async-start | bytes 2621440 | tf_op jit(solution)/shard_map/reduce_scatter | solution.py:158
  245.0 10.5 %copy-start.9 = (f32[256,32]{0,1:T(8,128)S(1)}, f32[256,32]{0,1:T(8,128)}, u32[]{:S(2)}) copy-start(f32[256,32]{0,1:T(8,128)} %copy.75) | copy-start | bytes 98308
  261.5 56.2 %copy-start.1 = (bf16[256,4096]{1,0:T(8,128)(2,1)S(1)}, bf16[256,4096]{1,0:T(8,128)(2,1)}, u32[]{:S(2)}) copy-start(bf16[256,4096]{1,0:T(8,128)(2,1)} %param.12) | copy-start | bytes 6291460
Sparse Core Ops, SparseCore 0:
  9.9 92.5 all-gather.7
  116.0 36.7 all-gather.11
  182.3 54.3 all-gather.9
  273.8 43.8 reduce-scatter.1
where the time goes:
time: 325 us; the launch traced here: 324 us
  waiting for transfers between devices  192 us (59%)
  matrix products  57.5 us (18%)
  other arithmetic  25.4 us (8%)
  blocking collectives  17.8 us (5%)
  local copies, waits for them, and re-layouts  17.1 us (5%)
  between operations  14 us (4%)
    all_gather x1, waiting for transfers between devices, body(): full_weight = lax.all_gather(x_weight, 'seq', axis=0, tiled=True)  90.6 us
    reduce_scatter x1, waiting for transfers between devices, body(): lax.psum_scatter(partial_sums.astype(jnp.bfloat16), 'head', scatter_dimen...  44 us
    all_gather x1, waiting for transfers between devices, entering(): pieces = jax.tree.map(lambda part: lax.all_gather(part, axis), value)  41.1 us
    all_gather x1, waiting for transfers between devices, prefix_2(): lax.all_gather(part.astype(kind), axis)  15.4 us
    dot_general x1, matrix products, body(): jnp.einsum('tk,dk->td', x_grad, full_weight, preferred_element_type=jnp.f...  12.1 us
    select_n x8, other arithmetic, prefix_hop(): return jax.tree.map(lambda a, b: jnp.where(reached, a, b), new, before)  10.4 us
    select_n x7, other arithmetic, entering_hop(): jnp.where(position < mine, new, old)  10.3 us
    all_gather x1, blocking collectives, entering(): pieces = jax.tree.map(lambda part: lax.all_gather(part, axis), value)  8.92 us
  transfers between devices with their start and end apart: 4, of which 4 were waited for; matrix products, arithmetic and copies ran while one was open for 6% of the time, Pallas kernels for 0%

commit v1 on v0

--- a/solution.py
+++ b/solution.py
@@ -70,7 +70,12 @@
     head_count = log_decay.shape[1]
     width_here = x_weight.shape[1]
     block_count = token_count // SPAN
-    full_weight = lax.all_gather(x_weight, "seq", axis=0, tiled=True)
+    ring = [x_weight]
+    for hop in range(7):
+        ring.append(lax.ppermute(ring[-1], "seq", [(dev, (dev + 1) % 8) for dev in range(8)]))
+    full_weight = jnp.roll(
+        jnp.concatenate(ring[::-1], axis=0), (lax.axis_index("seq") + 1) * ring[0].shape[0], axis=0
+    )
     x_sums = jnp.dot(inputs, full_weight, preferred_element_type=jnp.float32)
     x_values = x_sums.astype(jnp.bfloat16)
     first_head = lax.axis_index("head") * head_count

time: 325 us -> 457 us (1.41)
  waiting for transfers between devices: 192 us -> 282 us
  local copies, waits for them, and re-layouts: 17.1 us -> 58.7 us
    ppermute x0 -> x7, waiting for transfers between devices: none -> 181 us  [body(): lax.ppermute(ring[-1], 'seq', [(dev, (dev + 1) % 8) for dev in range(8)])]
    all_gather x1 -> x0, waiting for transfers between devices: 90.6 us -> none  [body(): full_weight = lax.all_gather(x_weight, 'seq', axis=0, tiled=True)]
    unnamed x25 -> x60, local copies, waits for them, and re-layouts: 3.12 us -> 43 us
  transfers between devices with their start and end apart: 4 -> 10, of which waited for: 4 -> 10; matrix products, arithmetic and copies ran while one was open for 6% -> 4% of each run, Pallas kernels for 0% -> 0%
where the time goes in v1:
time: 457 us; the launch traced here: 455 us
  waiting for transfers between devices  282 us (62%)
  local copies, waits for them, and re-layouts  58.7 us (13%)
  matrix products  55.8 us (12%)
  other arithmetic  25.3 us (6%)
  blocking collectives  18.6 us (4%)
  between operations  14 us (3%)
    ppermute x7, waiting for transfers between devices, body(): lax.ppermute(ring[-1], 'seq', [(dev, (dev + 1) % 8) for dev in range(8)])  181 us
    reduce_scatter x1, waiting for transfers between devices, body(): lax.psum_scatter(partial_sums.astype(jnp.bfloat16), 'head', scatter_dimen...  44 us
    unnamed x60, local copies, waits for them, and re-layouts  43 us
    all_gather x1, waiting for transfers between devices, entering(): pieces = jax.tree.map(lambda part: lax.all_gather(part, axis), value)  41.1 us
    all_gather x1, waiting for transfers between devices, prefix_2(): lax.all_gather(part.astype(kind), axis)  15.6 us
    dot_general x1, matrix products, body(): jnp.einsum('tk,dk->td', x_grad, full_weight, preferred_element_type=jnp.f...  12.1 us
    select_n x8, other arithmetic, prefix_hop(): return jax.tree.map(lambda a, b: jnp.where(reached, a, b), new, before)  10.4 us
    select_n x7, other arithmetic, entering_hop(): jnp.where(position < mine, new, old)  10.2 us
  transfers between devices with their start and end apart: 10, of which 10 were waited for; matrix products, arithmetic and copies ran while one was open for 4% of the time, Pallas kernels for 0%

profile of v1, /device:TPU:0, one launch (start us, length us, event | category | flops | bytes accessed | tf_op | source)
XLA Modules:
  0.0 455.4 jit_solution(2814309517143871245)
XLA Ops:
  7.7 26.8 %collective-permute-done = bf16[512,2048]{1,0:T(8,128)(2,1)S(1)} collective-permute-done((bf16[512,2048]{1,0:T(8,128)(2,1)}, bf16[512,2048]{1,0:T(8,128)(2,1)S(1)}, u32[]{:S(2)}, u32[]{:S(2)}) %collective-permute-start) | collective-permute-done | bytes 2097184 | tf_op jit(solution)/shard_map/ppermute | solution.py:75
  35.8 26.4 %collective-permute-done.1 = bf16[512,2048]{1,0:T(8,128)(2,1)S(1)} collective-permute-done((bf16[512,2048]{1,0:T(8,128)(2,1)S(1)}, bf16[512,2048]{1,0:T(8,128)(2,1)S(1)}, u32[]{:S(2)}, u32[]{:S(2)}) %collective-permute-start.1) | collective-permute-done | bytes 2097184 | tf_op jit(solution)/shard_map/ppermute | solution.py:75
  63.6 26.4 %collective-permute-done.2 = bf16[512,2048]{1,0:T(8,128)(2,1)S(1)} collective-permute-done((bf16[512,2048]{1,0:T(8,128)(2,1)S(1)}, bf16[512,2048]{1,0:T(8,128)(2,1)S(1)}, u32[]{:S(2)}, u32[]{:S(2)}) %collective-permute-start.2) | collective-permute-done | bytes 2097184 | tf_op jit(solution)/shard_map/ppermute | solution.py:75
  91.3 26.4 %collective-permute-done.3 = bf16[512,2048]{1,0:T(8,128)(2,1)S(1)} collective-permute-done((bf16[512,2048]{1,0:T(8,128)(2,1)S(1)}, bf16[512,2048]{1,0:T(8,128)(2,1)S(1)}, u32[]{:S(2)}, u32[]{:S(2)}) %collective-permute-start.3) | collective-permute-done | bytes 2097184 | tf_op jit(solution)/shard_map/ppermute | solution.py:75
  119.0 26.4 %collective-permute-done.4 = bf16[512,2048]{1,0:T(8,128)(2,1)S(1)} collective-permute-done((bf16[512,2048]{1,0:T(8,128)(2,1)S(1)}, bf16[512,2048]{1,0:T(8,128)(2,1)S(1)}, u32[]{:S(2)}, u32[]{:S(2)}) %collective-permute-start.4) | collective-permute-done | bytes 2097184 | tf_op jit(solution)/shard_map/ppermute | solution.py:75
  146.7 26.5 %collective-permute-done.5 = bf16[512,2048]{1,0:T(8,128)(2,1)} collective-permute-done((bf16[512,2048]{1,0:T(8,128)(2,1)S(1)}, bf16[512,2048]{1,0:T(8,128)(2,1)}, u32[]{:S(2)}, u32[]{:S(2)}) %collective-permute-start.5) | collective-permute-done | bytes 2097184 | tf_op jit(solution)/shard_map/ppermute | solution.py:75
  177.5 22.4 %collective-permute-done.6 = bf16[512,2048]{1,0:T(8,128)(2,1)} collective-permute-done((bf16[512,2048]{1,0:T(8,128)(2,1)}, bf16[512,2048]{1,0:T(8,128)(2,1)}, u32[]{:S(2)}, u32[]{:S(2)}) %collective-permute-start.6) | collective-permute-done | bytes 2097184 | tf_op jit(solution)/shard_map/ppermute | solution.py:75
  199.8 3.2 constant_dynamic-update-slice_fusion.15
  203.0 3.3 constant_dynamic-update-slice_fusion.14
  219.6 3.2 constant_dynamic-update-slice_fusion.7
  222.7 3.2 constant_dynamic-update-slice_fusion.6
  234.8 8.5 %fusion.9 = bf16[2048,256]{1,0:T(8,128)(2,1)S(1)} fusion(bf16[256,4096]{1,0:T(8,128)(2,1)S(1)} %copy-done, bf16[8192,2048]{1,0:T(8,128)(2,1)} %constant_dynamic-update-slice_fusion, s32[]{:T(128)S(6)} %select_n.77), kind=kOutput, calls=%fused_computation.18 | convolution fusion | flops 4295491584 | bytes 19922948 | tf_op jit(solution)/shard_map/dot_general | solution.py:79
  243.4 2.7 fusion.42
  246.2 9.7 %all-gather.3 = bf16[8,1,32]{2,1,0:T(2,128)(2,1)S(1)} all-gather(bf16[1,1,32]{2,1,0:T(2,128)(2,1)S(1)} %get-tuple-element.325), channel_id=5, replica_groups=mesh['seq'=8,'head'=4] {'seq'}, dimensions={0}, use_global_device_ids=true | all-gather | bytes 576 | tf_op jit(solution)/shard_map/all_gather | solution.py:17
  257.7 6.0 %multiply_convert_fusion = bf16[32,256,256]{2,1,0:T(8,128)(2,1)S(1)} fusion(f32[32,256]{1,0:T(8,128)S(1)} %copy.69, pred[256,256]{1,0:T(8,128)(4,1)S(1)} %iota_compare_fusion, bf16[256,32,128]{2,1,0:T(8,128)(2,1)S(1)} %copy-done.16, bf16[256,32,128]{2,1,0:T(8,128)(2,1)S(1)} %convert_bitcast_fusion.1), kind=kOutput, calls=%fused_computation.10 | convolution fusion | flops 547356672 | bytes 8486912 | tf_op jit(solution)/shard_map/while/body/eval_jaxpr/thn,shn->hts/dot_general | solution.py:54
  263.7 1.9 copy-done.3
  265.7 2.8 fusion.57
  268.4 15.6 %all-gather.9.cloned.1.call-done = bf16[256,64,128]{2,1,0:T(8,128)(2,1)} async-done(((bf16[32,64,128]{2,1,0:T(8,128)(2,1)}), bf16[256,64,128]{2,1,0:T(8,128)(2,1)}) %all-gather.9.cloned.1.call-update) | async-done | bytes 4194320 | tf_op jit(solution)/shard_map/all_gather | solution.py:17
  284.1 10.7 %while.19 = (s32[]{:T(128)}, f32[32,64,128]{2,1,0:T(8,128)S(1)}, s32[]{:T(128)}, bf16[8,32]{1,0:T(8,128)(2,1)S(1)}, bf16[8,32,64,128]{3,2,1,0:T(8,128)(2,1)}, /*index=5*/s32[]{:T(128)}, s32[]{:T(128)}) while((s32[]{:T(128)}, f32[32,64,128]{2,1,0:T(8,128)S(1)}, s32[]{:T(128)}, bf16[8,32]{1,0:T(8,128)(2,1)S(1)}, ...), condition=%wide.region_6.7_spmd.clone, body=%wide.region_5.6_spmd.clone.sunk | while | flops 1310756 | bytes 2621865 | solution.py:34
  294.7 6.3 %fusion.16 = f32[256,32,64]{0,2,1:T(8,128)} fusion(bf16[256,32,64]{0,2,1:T(8,128)(2,1)S(1)} %bitcast.105, f32[32,64,256]{2,1,0:T(8,128)} %fusion.57, f32[32,64,128]{2,1,0:T(8,128)S(1)} %get-tuple-element.254, bf16[256,32,128]{2,1,0:T(8,128)(2,1)} %copy-done.2, f32[256,32]{0,1:T(8,128)S(1)} %copy.75, f32[32]{0:T(128)S(1)} %copy-done.21), kind=kOutput, calls=%fused_computation.23 | convolution fusion | flops 807927808 | bytes 8421504 | tf_op jit(solution)/shard_map/while/body/eval_jaxpr/thn,hpn->thp/dot_general | solution.py:133
  301.1 2.0 copy.78
  303.1 3.9 fusion.14
  307.0 1.9 copy.63
  308.9 4.5 fusion.34
  313.5 8.9 %all-gather = f32[8,1,32]{2,1,0:T(1,128)S(1)} all-gather(f32[1,1,32]{2,1,0:T(1,128)S(1)} %get-tuple-element.327), channel_id=2, replica_groups=mesh['seq'=8,'head'=4] {'seq'}, dimensions={0}, use_global_device_ids=true | all-gather | bytes 1152 | tf_op jit(solution)/shard_map/all_gather | solution.py:39
  322.4 4.5 fusion.47
  326.9 41.1 %all-gather.7.cloned.1.call-done = f32[256,64,128]{2,1,0:T(8,128)} async-done(((f32[32,64,128]{2,1,0:T(8,128)}), f32[256,64,128]{2,1,0:T(8,128)}) %all-gather.7.cloned.1.call-update) | async-done | bytes 8388624 | tf_op jit(solution)/shard_map/all_gather | solution.py:39
  368.0 8.3 %rev.7 = f32[8,32,64,128]{3,2,1,0:T(8,128)} reverse(f32[8,32,64,128]{3,2,1,0:T(8,128)} %bitcast.101), dimensions={0} | reverse | bytes 16777216 | tf_op jit(solution)/shard_map/rev | solution.py:40
  376.3 10.5 %while.18 = (s32[]{:T(128)}, f32[32,64,128]{2,1,0:T(8,128)S(1)}, s32[]{:T(128)}, f32[8,32]{1,0:T(8,128)S(1)}, f32[8,32,64,128]{3,2,1,0:T(8,128)}, /*index=5*/s32[]{:T(128)}, s32[]{:T(128)}) while((s32[]{:T(128)}, f32[32,64,128]{2,1,0:T(8,128)S(1)}, s32[]{:T(128)}, f32[8,32]{1,0:T(8,128)S(1)}, f32[8,32,64,128]{3,2,1,0:T(8,128)}, ...), condition=%wide.region_3.4_spmd.clone, body=%wide.region_2.3_spmd.clone.sunk | while | flops 1048580 | bytes 3146217 | solution.py:50
  386.8 5.9 %fusion.25 = bf16[256,32,64]{0,2,1:T(8,128)(2,1)} fusion(f32[32,64,256]{2,1,0:T(8,128)} %fusion.47, f32[256,32,64]{0,2,1:T(8,128)S(1)} %bitcast.100, f32[32,64,128]{2,1,0:T(8,128)S(1)} %get-tuple-element.253, bf16[256,32,128]{2,1,0:T(8,128)(2,1)} %copy-done.15, f32[32]{0:T(128)S(1)} %copy-done.21, f32[256,32]{0,1:T(8,128)S(1)} %copy-done.20), kind=kOutput, calls=%fused_computation.34 | convolution fusion | flops 807927808 | bytes 8421504 | tf_op jit(solution)/shard_map/while/body/eval_jaxpr/shn,hpn->shp/dot_general | solution.py:149
  392.7 12.1 %fusion.6 = bf16[256,4096]{1,0:T(8,128)(2,1)} fusion(bf16[256,2048]{0,1:T(8,128)(2,1)} %bitcast.110, bf16[8192,2048]{1,0:T(8,128)(2,1)} %constant_dynamic-update-slice_fusion, s32[]{:T(128)S(6)} %select_n.77), kind=kOutput, calls=%fused_computation.11 | convolution fusion | flops 4296015872 | bytes 19922948 | tf_op jit(solution)/shard_map/tk,dk->td/dot_general | solution.py:162
  404.8 44.0 %reduce-scatter.2.cloned.1.call-done = bf16[256,1024]{1,0:T(8,128)(2,1)} async-done(((bf16[256,4096]{1,0:T(8,128)(2,1)}), bf16[256,1024]{1,0:T(8,128)(2,1)}) %reduce-scatter.2.cloned.1.call-update) | async-done | bytes 524304 | tf_op jit(solution)/shard_map/reduce_scatter | solution.py:163
  (121 shorter events, 56.4 us)
Async XLA Ops:
  7.2 227.7 %copy-start = (bf16[256,4096]{1,0:T(8,128)(2,1)S(1)}, bf16[256,4096]{1,0:T(8,128)(2,1)}, u32[]{:S(2)}) copy-start(bf16[256,4096]{1,0:T(8,128)(2,1)} %param.12) | copy-start | bytes 6291460
  7.2 276.9 %all-gather.9.cloned.1.call-start = ((), (), s32[]{:S(2)}) async-start(), calls=%async_computation.3 | async-start | bytes 4718592 | tf_op jit(solution)/shard_map/all_gather | solution.py:17
  7.2 27.3 %collective-permute-start = (bf16[512,2048]{1,0:T(8,128)(2,1)}, bf16[512,2048]{1,0:T(8,128)(2,1)S(1)}, u32[]{:S(2)}, u32[]{:S(2)}) collective-permute-start(bf16[512,2048]{1,0:T(8,128)(2,1)} %param.13), channel_id=1, source_target_pairs={{0,4},{4,8},{8,12},{12,16},{16,20},{20,24},{24,28},{28,0},{1,5},{5... | collective-permute-start | bytes 6291464 | tf_op jit(solution)/shard_map/ppermute | solution.py:75
  34.5 1.3 copy-start.5
  35.8 26.4 %collective-permute-start.1 = (bf16[512,2048]{1,0:T(8,128)(2,1)S(1)}, bf16[512,2048]{1,0:T(8,128)(2,1)S(1)}, u32[]{:S(2)}, u32[]{:S(2)}) collective-permute-start(bf16[512,2048]{1,0:T(8,128)(2,1)S(1)} %collective-permute-done), channel_id=1, source_target_pairs={{0,4},{4,8},{8,12},{12,16},{16,20},{20,24},{24,28},{28,0},{1,5},{5... | collective-permute-start | bytes 6291464 | tf_op jit(solution)/shard_map/ppermute | solution.py:75
  62.2 1.4 copy-start.7
  63.6 26.4 %collective-permute-start.2 = (bf16[512,2048]{1,0:T(8,128)(2,1)S(1)}, bf16[512,2048]{1,0:T(8,128)(2,1)S(1)}, u32[]{:S(2)}, u32[]{:S(2)}) collective-permute-start(bf16[512,2048]{1,0:T(8,128)(2,1)S(1)} %collective-permute-done.1), channel_id=1, source_target_pairs={{0,4},{4,8},{8,12},{12,16},{16,20},{20,24},{24,28},{28,0},{1,5},{5... | collective-permute-start | bytes 6291464 | tf_op jit(solution)/shard_map/ppermute | solution.py:75
  89.9 1.4 copy-start.9
  91.3 26.4 %collective-permute-start.3 = (bf16[512,2048]{1,0:T(8,128)(2,1)S(1)}, bf16[512,2048]{1,0:T(8,128)(2,1)S(1)}, u32[]{:S(2)}, u32[]{:S(2)}) collective-permute-start(bf16[512,2048]{1,0:T(8,128)(2,1)S(1)} %collective-permute-done.2), channel_id=1, source_target_pairs={{0,4},{4,8},{8,12},{12,16},{16,20},{20,24},{24,28},{28,0},{1,5},{5... | collective-permute-start | bytes 6291464 | tf_op jit(solution)/shard_map/ppermute | solution.py:75
  117.7 1.3 copy-start.11
  119.0 26.4 %collective-permute-start.4 = (bf16[512,2048]{1,0:T(8,128)(2,1)S(1)}, bf16[512,2048]{1,0:T(8,128)(2,1)S(1)}, u32[]{:S(2)}, u32[]{:S(2)}) collective-permute-start(bf16[512,2048]{1,0:T(8,128)(2,1)S(1)} %collective-permute-done.3), channel_id=1, source_target_pairs={{0,4},{4,8},{8,12},{12,16},{16,20},{20,24},{24,28},{28,0},{1,5},{5... | collective-permute-start | bytes 6291464 | tf_op jit(solution)/shard_map/ppermute | solution.py:75
  145.3 1.3 copy-start.13
  146.7 26.5 %collective-permute-start.5 = (bf16[512,2048]{1,0:T(8,128)(2,1)S(1)}, bf16[512,2048]{1,0:T(8,128)(2,1)}, u32[]{:S(2)}, u32[]{:S(2)}) collective-permute-start(bf16[512,2048]{1,0:T(8,128)(2,1)S(1)} %collective-permute-done.4), channel_id=1, source_target_pairs={{0,4},{4,8},{8,12},{12,16},{16,20},{20,24},{24,28},{28,0},{1,5},{5... | collective-permute-start | bytes 6291464 | tf_op jit(solution)/shard_map/ppermute | solution.py:75
  173.2 26.7 %collective-permute-start.6 = (bf16[512,2048]{1,0:T(8,128)(2,1)}, bf16[512,2048]{1,0:T(8,128)(2,1)}, u32[]{:S(2)}, u32[]{:S(2)}) collective-permute-start(bf16[512,2048]{1,0:T(8,128)(2,1)} %collective-permute-done.5), channel_id=1, source_target_pairs={{0,4},{4,8},{8,12},{12,16},{16,20},{20,24},{24,28},{28,0},{1,5},{5... | collective-permute-start | bytes 6291464 | tf_op jit(solution)/shard_map/ppermute | solution.py:75
  177.5 65.9 %copy-start.15 = (bf16[256,32,128]{2,1,0:T(8,128)(2,1)}, bf16[256,32,128]{2,1,0:T(8,128)(2,1)S(1)}, u32[]{:S(2)}) copy-start(bf16[256,32,128]{2,1,0:T(8,128)(2,1)S(1)} %convert_bitcast_fusion) | copy-start | bytes 6291460
  203.0 3.3 copy-start.14
  206.4 2.3 copy-start.12
  208.7 2.3 copy-start.10
  211.1 2.3 copy-start.8
  213.4 2.3 copy-start.6
  215.7 2.3 copy-start.4
  234.8 8.5 %copy-start.19 = (f32[256,32]{0,1:T(8,128)S(1)}, f32[256,32]{0,1:T(8,128)}, u32[]{:S(2)}) copy-start(f32[256,32]{0,1:T(8,128)} %copy.71) | copy-start | bytes 98308
  243.4 12.7 %copy-start.18 = (bf16[256,8,128]{2,1,0:T(8,128)(2,1)S(1)}, bf16[256,8,128]{2,1,0:T(8,128)(2,1)}, u32[]{:S(2)}) copy-start(bf16[256,8,128]{2,1,0:T(8,128)(2,1)} %param.15) | copy-start | bytes 1572868
  246.1 121.9 %all-gather.7.cloned.1.call-start = ((), (), s32[]{:S(2)}) async-start(), calls=%async_computation.2 | async-start | bytes 9437184 | tf_op jit(solution)/shard_map/all_gather | solution.py:39
  256.1 1.6 copy-start.16
  257.7 6.0 %copy-start.2 = (bf16[256,32,128]{2,1,0:T(8,128)(2,1)}, bf16[256,32,128]{2,1,0:T(8,128)(2,1)S(1)}, u32[]{:S(2)}) copy-start(bf16[256,32,128]{2,1,0:T(8,128)(2,1)S(1)} %convert_bitcast_fusion.1) | copy-start | bytes 6291460
  263.7 2.0 copy-start.3
  284.1 10.7 %copy-start.21 = (f32[32]{0:T(128)S(1)}, f32[32]{0:T(128)}, u32[]{:S(2)}) copy-start(f32[32]{0:T(128)} %param.18) | copy-start | bytes 388
  301.1 2.0 copy-start.17
  313.4 135.4 %reduce-scatter.2.cloned.1.call-start = ((), (), s32[]{:S(2)}) async-start(), calls=%async_computation.1 | async-start | bytes 2621440 | tf_op jit(solution)/shard_map/reduce_scatter | solution.py:163
  376.3 10.5 %copy-start.20 = (f32[256,32]{0,1:T(8,128)S(1)}, f32[256,32]{0,1:T(8,128)}, u32[]{:S(2)}) copy-start(f32[256,32]{0,1:T(8,128)} %copy.71) | copy-start | bytes 98308
  392.7 56.1 %copy-start.1 = (bf16[256,4096]{1,0:T(8,128)(2,1)S(1)}, bf16[256,4096]{1,0:T(8,128)(2,1)}, u32[]{:S(2)}) copy-start(bf16[256,4096]{1,0:T(8,128)(2,1)} %param.12) | copy-start | bytes 6291460
Sparse Core Ops, SparseCore 0:
  246.2 37.7 all-gather.8
  313.6 54.3 all-gather.6
  404.9 43.8 reduce-scatter.1
